TPU v7x, 512 devices: a whole 4x4x16 slice. The times are simulated.
512 devices in a mesh: band: 8 (over y, core), space: 64 (over z, x).
Axes of the slice: x: 4, y: 4, z: 16, core: 2. Of those that a mesh axis runs over, the one named last changes fastest.
Arguments:
- snapshots: float32 [1152, 8, 32768], P(None, 'band', 'space'), may hold values from -6 to 6
- quad_weights: float32 [8, 32768], P('band', 'space'), may hold values from 0.2 to 9, as said below
- freq_bins: int32 [16], replicated, may hold values from 1 to 127, as said below
- block_starts: int32 [8], replicated, may hold values from 0 to 896, as said below
Outputs:
- factor: float32 [16, 2, 8, 8], P('band')
- modes: float32 [16, 2, 8, 8, 32768], P('band', None, None, None, 'space')
Inputs may be any that keep to these rules, and one draw needn't show every extreme that they name: `freq_bins`: distinct and increasing; the first is 1 and the last is 127. `block_starts`: Increasing; the first is 0 and the last is 896; consecutive starts differ by 64 to 192. `quad_weights`: Positive.
All inputs are finite; a program needn't handle non-finite values.
Results may differ from a plain program's by a relative error of at most 0.000075.
Values sent between devices are 32-bit elements; how exact they have to be, the bound alone decides.
A program may use at most 64 MiB of HBM per device.

v0:
```python
import math

import jax
import jax.numpy as jnp
from jax import lax
from jax.sharding import PartitionSpec as P

BLOCK = 256
NBLK = 8
NFREQ = 16
SLABS = 8


def from_partner(block, axis, apart):
    count = lax.axis_size(axis)
    route = []
    for low in range(count):
        high = low | 1 << apart
        if high != low and high < count:
            route += [(low, high), (high, low)]
    return lax.ppermute(block, axis, route)


def spectral_table(freq_bins, block_starts, total_times):
    moments = jnp.arange(total_times)
    offset = moments[None, :] - block_starts[:, None]
    inside = (offset >= 0) & (offset < BLOCK)
    position = offset.astype(jnp.float32)
    taper = 0.5 - 0.5 * jnp.cos(2.0 * math.pi * position / BLOCK)
    turns = jnp.mod(freq_bins[:, None, None] * offset[None, :, :], BLOCK).astype(jnp.float32)
    phase = 2.0 * math.pi * turns / BLOCK
    scaled = jnp.where(inside, taper, 0.0)[None] / math.sqrt(0.375 * BLOCK)
    table = jnp.stack([scaled * jnp.cos(phase), -scaled * jnp.sin(phase)], axis=1)
    return table.reshape(-1, total_times)


def spectra(snap_rows, weights, table):
    fluct = snap_rows - jnp.mean(snap_rows, axis=0, keepdims=True)
    coeffs = jnp.dot(
        table, fluct, precision=lax.Precision.HIGHEST, preferred_element_type=jnp.float32
    )
    return coeffs * jnp.sqrt(weights)[None, :]


def gram_local(coeffs, count):
    vectors = coeffs.reshape(coeffs.shape[0], 2 * coeffs.shape[2], -1)
    return jnp.einsum("fas,fbs->fab", vectors, vectors, precision=lax.Precision.HIGHEST) / count


def gram_split(moment):
    half = moment.shape[-1] // 2
    real_part = moment[:, :half, :half] + moment[:, half:, half:]
    imag_part = moment[:, :half, half:] - moment[:, half:, :half]
    return (real_part, imag_part)


def factor_pair(gram_real, gram_imag):
    order = gram_real.shape[-1]
    columns = jnp.arange(order)
    rows_real = []
    rows_imag = []
    for pivot_row in range(order):
        left_real = gram_real[:, pivot_row, :]
        left_imag = gram_imag[:, pivot_row, :]
        for earlier in range(pivot_row):
            coef_real = rows_real[earlier][:, pivot_row : pivot_row + 1]
            coef_imag = rows_imag[earlier][:, pivot_row : pivot_row + 1]
            left_real = left_real - (
                coef_real * rows_real[earlier] + coef_imag * rows_imag[earlier]
            )
            left_imag = left_imag - (
                coef_real * rows_imag[earlier] - coef_imag * rows_real[earlier]
            )
        pivot = jnp.sqrt(left_real[:, pivot_row : pivot_row + 1])
        rows_real.append(jnp.where(columns >= pivot_row, left_real / pivot, 0.0))
        rows_imag.append(jnp.where(columns > pivot_row, left_imag / pivot, 0.0))
    return (jnp.stack(rows_real, 1), jnp.stack(rows_imag, 1))


def invert_pair(fac_real, fac_imag):
    order = fac_real.shape[-1]
    identity = jnp.eye(order, dtype=fac_real.dtype)
    inv_real = [None] * order
    inv_imag = [None] * order
    for target in reversed(range(order)):
        acc_real = jnp.broadcast_to(identity[target], fac_real[:, 0, :].shape)
        acc_imag = jnp.zeros_like(acc_real)
        for later in range(target + 1, order):
            coef_real = fac_real[:, target, later : later + 1]
            coef_imag = fac_imag[:, target, later : later + 1]
            acc_real = acc_real - (coef_real * inv_real[later] - coef_imag * inv_imag[later])
            acc_imag = acc_imag - (coef_real * inv_imag[later] + coef_imag * inv_real[later])
        diagonal = fac_real[:, target, target : target + 1]
        inv_real[target] = acc_real / diagonal
        inv_imag[target] = acc_imag / diagonal
    return (jnp.stack(inv_real, 1), jnp.stack(inv_imag, 1))


def project(coeffs, inv_real, inv_imag):
    upper = jnp.stack([inv_real, inv_imag], 2)
    lower = jnp.stack([-inv_imag, inv_real], 2)
    kernel = jnp.stack([upper, lower], 1)
    flat = coeffs.reshape(coeffs.shape[0], 2, coeffs.shape[2], -1)
    result = jnp.einsum("fpacb,fpas->fcbs", kernel, flat, precision=lax.Precision.HIGHEST)
    return result.reshape(coeffs.shape)


def shards(snapshots, quad_weights, freq_bins, block_starts):
    total_times, local_slabs, slab_cells = snapshots.shape
    table = spectral_table(freq_bins, block_starts, total_times)
    coeffs = spectra(snapshots.reshape(total_times, -1), quad_weights.reshape(-1), table)
    coeffs = coeffs.reshape(NFREQ, 2, NBLK, local_slabs, slab_cells)
    count = SLABS * slab_cells * lax.axis_size("space")
    grouped = lax.all_to_all(coeffs, "band", split_axis=0, concat_axis=3, tiled=True)
    moment = gram_local(grouped, count)
    for level in range(lax.axis_size("space").bit_length() - 1):
        moment = moment + from_partner(moment, "space", level)
    fac_real, fac_imag = factor_pair(*gram_split(moment))
    modes = project(grouped, *invert_pair(fac_real, fac_imag))
    factor = jnp.stack([fac_real, fac_imag], 1)
    return (factor, modes)


def solution(mesh):
    placed = (P(None, "band", "space"), P("band", "space"), P(), P())
    return jax.shard_map(
        shards,
        mesh=mesh,
        in_specs=placed,
        out_specs=(P("band", None, None, None), P("band", None, None, None, "space")),
        check_vma=False,
    )
```

profile of v0, /device:TPU:8, one launch (start us, length us, event | category | flops | bytes accessed | tf_op | source)
XLA Modules:
  0.0 95.0 jit_solution(8340031226625557543)
XLA Ops:
  0.6 1.0 %select_multiply_fusion = (f32[8,1152]{1,0:T(8,128)S(1)}, f32[8,1152]{1,0:T(8,128)S(1)}) fusion(s32[8]{0:T(128)} %param.7), kind=kLoop, calls=%fused_computation.17 | loop fusion | flops 101376 | bytes 73760 | tf_op jit(solution)/shard_map/div | solution.py:32
  1.7 0.7 iota_subtract_fusion
  2.4 4.0 %reduce_sum.9 = f32[512]{0:T(512)S(1)} reduce(f32[1152,1,512]{2,1,0:T(1,128)} %param.4, f32[]{:T(128)} %constant.21.clone.1), dimensions={0,1}, to_apply=%region_0.1 | reduce | flops 589312 | bytes 2361348 | tf_op jit(solution)/shard_map/reduce_sum | solution.py:38
  6.5 1.7 %broadcast_subtract_fusion = f32[1152,1,512]{2,1,0:T(1,128)S(1)} fusion(f32[1152,1,512]{2,1,0:T(1,128)S(1)} %copy-done, f32[512]{0:T(512)S(1)} %broadcast_multiply_fusion), kind=kLoop, calls=%fused_computation.5 | loop fusion | flops 589824 | bytes 4720640 | tf_op jit(solution)/shard_map/sub | solution.py:38
  8.2 2.4 %cosine_multiply_fusion = (f32[16,1,8,1152]{3,2,1,0:T(8,128)S(1)}, f32[16,1,8,1152]{3,2,1,0:T(8,128)S(1)}) fusion(s32[8,1152]{1,0:T(8,128)S(1)} %iota_subtract_fusion, s32[16]{0:T(128)S(1)} %copy-done.2, f32[8,1152]{1,0:T(8,128)S(1)} %get-tuple-element.204, f32[8,1152]{1,0:T(8,128)S(1)} %get-tuple-element.205), kind=kLoop, calls=%fused_computation.16 | loop fusion | flops 2359296 | bytes 1290304 | tf_op jit(solution)/shard_map/mul | solution.py:33
  10.7 3.1 %fusion.3 = f32[256,512]{1,0:T(8,128)} fusion(f32[256,1152]{1,0:T(8,128)S(1)} %bitcast.76, f32[1152,1,512]{2,1,0:T(1,128)S(1)} %broadcast_subtract_fusion, f32[512]{0:T(512)S(1)} %bitcast.90), kind=kOutput, calls=%fused_computation.3 | convolution fusion | flops 1812070400 | bytes 4065280 | tf_op jit(solution)/shard_map/dot_general | solution.py:39
  13.9 9.2 %all-to-all-start = ((f32[16,2,8,1,512]{4,2,1,3,0:T(8,128)}), f32[16,2,8,1,512]{4,2,1,3,0:T(8,128)S(1)}, u32[]{:S(2)}, u32[]{:S(2)}) async-start(f32[16,2,8,1,512]{4,2,1,3,0:T(8,128)} %bitcast.3), calls=%async_computation | async-start | bytes 1048576 | tf_op jit(solution)/shard_map/all_to_all | solution.py:114
  23.1 8.9 %all-to-all-done = f32[16,2,8,1,512]{4,2,1,3,0:T(8,128)S(1)} async-done(((f32[16,2,8,1,512]{4,2,1,3,0:T(8,128)}), f32[16,2,8,1,512]{4,2,1,3,0:T(8,128)S(1)}, u32[]{:S(2)}, u32[]{:S(2)}) %all-to-all-start) | async-done | bytes 524320 | tf_op jit(solution)/shard_map/all_to_all | solution.py:114
  32.0 0.8 convolution_multiply_fusion
  32.8 1.9 %collective-permute-start = (f32[2,16,16]{2,1,0:T(8,128)S(1)}, f32[2,16,16]{2,1,0:T(8,128)S(1)}, u32[]{:S(2)}, u32[]{:S(2)}) collective-permute-start(f32[2,16,16]{2,1,0:T(8,128)S(1)} %convolution_multiply_fusion), channel_id=1, source_target_pairs={{0,1},{1,0},{2,3},{3,2},{4,5},{5,4},{6,7},{7,6},{8,9},{9,8},{10,11... | collective-permute-start | bytes 6152 | tf_op jit(solution)/shard_map/ppermute | solution.py:21
  34.8 3.7 %collective-permute-done = f32[2,16,16]{2,1,0:T(8,128)S(1)} collective-permute-done((f32[2,16,16]{2,1,0:T(8,128)S(1)}, f32[2,16,16]{2,1,0:T(8,128)S(1)}, u32[]{:S(2)}, u32[]{:S(2)}) %collective-permute-start) | collective-permute-done | bytes 2080 | tf_op jit(solution)/shard_map/ppermute | solution.py:21
  38.5 1.9 %collective-permute-start.1 = (f32[2,16,16]{2,1,0:T(8,128)S(1)}, f32[2,16,16]{2,1,0:T(8,128)S(1)}, u32[]{:S(2)}, u32[]{:S(2)}) collective-permute-start(f32[2,16,16]{2,1,0:T(8,128)S(1)} %add.1551), channel_id=1, source_target_pairs={{0,2},{2,0},{1,3},{3,1},{4,6},{6,4},{5,7},{7,5},{8,10},{10,8},{9,1... | collective-permute-start | bytes 6152 | tf_op jit(solution)/shard_map/ppermute | solution.py:21
  40.4 5.2 %collective-permute-done.1 = f32[2,16,16]{2,1,0:T(8,128)S(1)} collective-permute-done((f32[2,16,16]{2,1,0:T(8,128)S(1)}, f32[2,16,16]{2,1,0:T(8,128)S(1)}, u32[]{:S(2)}, u32[]{:S(2)}) %collective-permute-start.1) | collective-permute-done | bytes 2080 | tf_op jit(solution)/shard_map/ppermute | solution.py:21
  45.6 1.9 %collective-permute-start.2 = (f32[2,16,16]{2,1,0:T(8,128)S(1)}, f32[2,16,16]{2,1,0:T(8,128)S(1)}, u32[]{:S(2)}, u32[]{:S(2)}) collective-permute-start(f32[2,16,16]{2,1,0:T(8,128)S(1)} %add.1552), channel_id=1, source_target_pairs={{0,4},{4,0},{1,5},{5,1},{2,6},{6,2},{3,7},{7,3},{8,12},{12,8},{9,1... | collective-permute-start | bytes 6152 | tf_op jit(solution)/shard_map/ppermute | solution.py:21
  47.5 3.7 %collective-permute-done.2 = f32[2,16,16]{2,1,0:T(8,128)S(1)} collective-permute-done((f32[2,16,16]{2,1,0:T(8,128)S(1)}, f32[2,16,16]{2,1,0:T(8,128)S(1)}, u32[]{:S(2)}, u32[]{:S(2)}) %collective-permute-start.2) | collective-permute-done | bytes 2080 | tf_op jit(solution)/shard_map/ppermute | solution.py:21
  51.2 1.9 %collective-permute-start.3 = (f32[2,16,16]{2,1,0:T(8,128)S(1)}, f32[2,16,16]{2,1,0:T(8,128)S(1)}, u32[]{:S(2)}, u32[]{:S(2)}) collective-permute-start(f32[2,16,16]{2,1,0:T(8,128)S(1)} %add.1553), channel_id=1, source_target_pairs={{0,8},{8,0},{1,9},{9,1},{2,10},{10,2},{3,11},{11,3},{4,12},{12,4},... | collective-permute-start | bytes 6152 | tf_op jit(solution)/shard_map/ppermute | solution.py:21
  53.1 4.6 %collective-permute-done.3 = f32[2,16,16]{2,1,0:T(8,128)S(1)} collective-permute-done((f32[2,16,16]{2,1,0:T(8,128)S(1)}, f32[2,16,16]{2,1,0:T(8,128)S(1)}, u32[]{:S(2)}, u32[]{:S(2)}) %collective-permute-start.3) | collective-permute-done | bytes 2080 | tf_op jit(solution)/shard_map/ppermute | solution.py:21
  57.7 5.1 %collective-permute-start.4 = (f32[2,16,16]{2,1,0:T(8,128)S(1)}, f32[2,16,16]{2,1,0:T(8,128)S(1)}, u32[]{:S(2)}, u32[]{:S(2)}) collective-permute-start(f32[2,16,16]{2,1,0:T(8,128)S(1)} %add.1554), channel_id=1, source_target_pairs={{0,16},{16,0},{1,17},{17,1},{2,18},{18,2},{3,19},{19,3},{4,20},{20... | collective-permute-start | bytes 6152 | tf_op jit(solution)/shard_map/ppermute | solution.py:21
  62.9 4.4 %collective-permute-done.4 = f32[2,16,16]{2,1,0:T(8,128)S(1)} collective-permute-done((f32[2,16,16]{2,1,0:T(8,128)S(1)}, f32[2,16,16]{2,1,0:T(8,128)S(1)}, u32[]{:S(2)}, u32[]{:S(2)}) %collective-permute-start.4) | collective-permute-done | bytes 2080 | tf_op jit(solution)/shard_map/ppermute | solution.py:21
  67.3 11.4 %collective-permute-start.5 = (f32[2,16,16]{2,1,0:T(8,128)S(1)}, f32[2,16,16]{2,1,0:T(8,128)S(1)}, u32[]{:S(2)}, u32[]{:S(2)}) collective-permute-start(f32[2,16,16]{2,1,0:T(8,128)S(1)} %add.1555), channel_id=1, source_target_pairs={{0,32},{32,0},{1,33},{33,1},{2,34},{34,2},{3,35},{35,3},{4,36},{36... | collective-permute-start | bytes 6152 | tf_op jit(solution)/shard_map/ppermute | solution.py:21
  78.7 2.9 %collective-permute-done.5 = f32[2,16,16]{2,1,0:T(8,128)S(1)} collective-permute-done((f32[2,16,16]{2,1,0:T(8,128)S(1)}, f32[2,16,16]{2,1,0:T(8,128)S(1)}, u32[]{:S(2)}, u32[]{:S(2)}) %collective-permute-start.5) | collective-permute-done | bytes 2080 | tf_op jit(solution)/shard_map/ppermute | solution.py:21
  81.7 0.1 sqrt_reduce_fusion.7
  81.9 0.3 slice_reduce_fusion.77
  82.2 0.3 slice_reduce_fusion.76
  82.6 0.2 sqrt_reduce_fusion.6
  82.9 0.3 slice_reduce_fusion.75
  83.1 0.3 slice_reduce_fusion.74
  83.5 0.2 sqrt_reduce_fusion.5
  83.7 0.3 slice_reduce_fusion.73
  84.0 0.3 slice_reduce_fusion.72
  84.3 0.2 sqrt_reduce_fusion.4
  84.6 0.2 slice_reduce_fusion.71
  84.9 0.2 slice_reduce_fusion.70
  85.2 0.2 sqrt_reduce_fusion.3
  85.4 0.2 slice_reduce_fusion.69
  85.7 0.2 slice_reduce_fusion.68
  86.1 0.2 sqrt_reduce_fusion.2
  86.3 0.2 slice_reduce_fusion.67
  86.6 0.2 slice_reduce_fusion.66
  87.0 0.2 sqrt_reduce_fusion.1
  87.2 0.2 slice_reduce_fusion.65
  87.5 0.2 slice_reduce_fusion.64
  87.8 0.2 sqrt_reduce_fusion
  88.0 0.3 broadcast_select_fusion.2
  88.3 0.2 slice_reduce_fusion.63
  88.5 0.2 slice_reduce_fusion.56
  88.6 0.2 slice_reduce_fusion.62
  88.8 0.2 slice_reduce_fusion.61
  89.0 0.2 slice_reduce_fusion.60
  89.2 0.2 slice_reduce_fusion.59
  89.3 0.2 slice_reduce_fusion.58
  89.5 0.2 slice_reduce_fusion.54
  89.7 0.2 slice_reduce_fusion.13
  89.9 0.2 slice_reduce_fusion.25
  90.1 0.2 slice_reduce_fusion.35
  90.3 0.2 slice_reduce_fusion.43
  90.4 0.2 slice_reduce_fusion.49
  90.6 0.2 slice_reduce_fusion.53
  90.8 0.2 slice_reduce_fusion.55
  91.0 0.3 subtract_divide_fusion
  92.1 0.1 subtract_divide_fusion.1
  92.5 0.6 fusion.12
  93.2 1.1 %copy.45 = f32[2,2,8,8,512]{4,3,2,1,0:T(8,128)} copy(f32[2,2,8,8,512]{4,2,3,1,0:T(8,128)S(1)} %bitcast.78) | data formatting | bytes 1048576
  94.4 0.6 copy.44
  (68 shorter events, 3.1 us)
Async XLA Ops:
  0.6 5.8 %copy-start = (f32[1152,1,512]{2,1,0:T(1,128)S(1)}, f32[1152,1,512]{2,1,0:T(1,128)}, u32[]{:S(2)}) copy-start(f32[1152,1,512]{2,1,0:T(1,128)} %param.4) | copy-start | bytes 7077892
  6.5 1.7 %copy-start.1 = (f32[1,512]{1,0:T(1,128)S(1)}, f32[1,512]{1,0:T(1,128)}, u32[]{:S(2)}) copy-start(f32[1,512]{1,0:T(1,128)} %param.5) | copy-start | bytes 6148
  6.5 1.8 %copy-start.2 = (s32[16]{0:T(128)S(1)}, s32[16]{0:T(128)}, u32[]{:S(2)}) copy-start(s32[16]{0:T(128)} %param.6) | copy-start | bytes 196
  13.9 18.1 %all-to-all-start = ((f32[16,2,8,1,512]{4,2,1,3,0:T(8,128)}), f32[16,2,8,1,512]{4,2,1,3,0:T(8,128)S(1)}, u32[]{:S(2)}, u32[]{:S(2)}) async-start(f32[16,2,8,1,512]{4,2,1,3,0:T(8,128)} %bitcast.3), calls=%async_computation | async-start | bytes 1048576 | tf_op jit(solution)/shard_map/all_to_all | solution.py:114
  32.8 5.6 %collective-permute-start = (f32[2,16,16]{2,1,0:T(8,128)S(1)}, f32[2,16,16]{2,1,0:T(8,128)S(1)}, u32[]{:S(2)}, u32[]{:S(2)}) collective-permute-start(f32[2,16,16]{2,1,0:T(8,128)S(1)} %convolution_multiply_fusion), channel_id=1, source_target_pairs={{0,1},{1,0},{2,3},{3,2},{4,5},{5,4},{6,7},{7,6},{8,9},{9,8},{10,11... | collective-permute-start | bytes 6152 | tf_op jit(solution)/shard_map/ppermute | solution.py:21
  38.5 7.1 %collective-permute-start.1 = (f32[2,16,16]{2,1,0:T(8,128)S(1)}, f32[2,16,16]{2,1,0:T(8,128)S(1)}, u32[]{:S(2)}, u32[]{:S(2)}) collective-permute-start(f32[2,16,16]{2,1,0:T(8,128)S(1)} %add.1551), channel_id=1, source_target_pairs={{0,2},{2,0},{1,3},{3,1},{4,6},{6,4},{5,7},{7,5},{8,10},{10,8},{9,1... | collective-permute-start | bytes 6152 | tf_op jit(solution)/shard_map/ppermute | solution.py:21
  45.6 5.6 %collective-permute-start.2 = (f32[2,16,16]{2,1,0:T(8,128)S(1)}, f32[2,16,16]{2,1,0:T(8,128)S(1)}, u32[]{:S(2)}, u32[]{:S(2)}) collective-permute-start(f32[2,16,16]{2,1,0:T(8,128)S(1)} %add.1552), channel_id=1, source_target_pairs={{0,4},{4,0},{1,5},{5,1},{2,6},{6,2},{3,7},{7,3},{8,12},{12,8},{9,1... | collective-permute-start | bytes 6152 | tf_op jit(solution)/shard_map/ppermute | solution.py:21
  51.2 6.5 %collective-permute-start.3 = (f32[2,16,16]{2,1,0:T(8,128)S(1)}, f32[2,16,16]{2,1,0:T(8,128)S(1)}, u32[]{:S(2)}, u32[]{:S(2)}) collective-permute-start(f32[2,16,16]{2,1,0:T(8,128)S(1)} %add.1553), channel_id=1, source_target_pairs={{0,8},{8,0},{1,9},{9,1},{2,10},{10,2},{3,11},{11,3},{4,12},{12,4},... | collective-permute-start | bytes 6152 | tf_op jit(solution)/shard_map/ppermute | solution.py:21
  57.7 9.5 %collective-permute-start.4 = (f32[2,16,16]{2,1,0:T(8,128)S(1)}, f32[2,16,16]{2,1,0:T(8,128)S(1)}, u32[]{:S(2)}, u32[]{:S(2)}) collective-permute-start(f32[2,16,16]{2,1,0:T(8,128)S(1)} %add.1554), channel_id=1, source_target_pairs={{0,16},{16,0},{1,17},{17,1},{2,18},{18,2},{3,19},{19,3},{4,20},{20... | collective-permute-start | bytes 6152 | tf_op jit(solution)/shard_map/ppermute | solution.py:21
  67.3 14.3 %collective-permute-start.5 = (f32[2,16,16]{2,1,0:T(8,128)S(1)}, f32[2,16,16]{2,1,0:T(8,128)S(1)}, u32[]{:S(2)}, u32[]{:S(2)}) collective-permute-start(f32[2,16,16]{2,1,0:T(8,128)S(1)} %add.1555), channel_id=1, source_target_pairs={{0,32},{32,0},{1,33},{33,1},{2,34},{34,2},{3,35},{35,3},{4,36},{36... | collective-permute-start | bytes 6152 | tf_op jit(solution)/shard_map/ppermute | solution.py:21
where the time goes:
time: 95.4 us; the launch traced here: 95 us
  starting transfers between devices  33.4 us (35%)
  waiting for transfers between devices  33.3 us (35%)
  other arithmetic  12.5 us (13%)
  local copies, waits for them, and re-layouts  10.3 us (11%)
  matrix products  4.59 us (5%)
  between operations  1 us (1%)
    ppermute x6, waiting for transfers between devices, from_partner(): return lax.ppermute(block, axis, route)  24.5 us
    ppermute x6, starting transfers between devices, from_partner(): return lax.ppermute(block, axis, route)  24.2 us
    all_to_all x1, starting transfers between devices, shards(): lax.all_to_all(coeffs, 'band', split_axis=0, concat_axis=3, tiled=True)  9.2 us
    all_to_all x1, waiting for transfers between devices, shards(): lax.all_to_all(coeffs, 'band', split_axis=0, concat_axis=3, tiled=True)  8.85 us
    reduce_sum x1, other arithmetic, spectra(): fluct = snap_rows - jnp.mean(snap_rows, axis=0, keepdims=True)  4.05 us
    dot_general x1, matrix products, spectra(): jnp.dot(table, fluct, precision=lax.Precision.HIGHEST, preferred_element_...  3.13 us
    mul x1, other arithmetic, spectral_table(): scaled * jnp.cos(phase)  2.4 us
  transfers between devices with their start and end apart: 7, of which 7 were waited for; matrix products, arithmetic and copies ran while one was open for 0% of the time, Pallas kernels for 0%

commit v1 on v0

v1 whole, which is shorter than its diff:
```python
import functools
import math

import jax
import jax.numpy as jnp
from jax import lax
from jax.experimental import pallas as pl
from jax.experimental.pallas import tpu as pltpu
from jax.sharding import PartitionSpec as P

BLOCK = 256
NBLK = 8
NFREQ = 16
SLABS = 8
TIMES = 1152
CELLS = 512
LANES = 128
TILES = CELLS // LANES
ROWS = 2 * NFREQ * NBLK
HALF = NFREQ * NBLK
ALONG_X = 4
MESH = pl.DeviceIdType.MESH
CHUNKS = 4


def turn_parts(turns):
    quadrant = jnp.bitwise_and(jnp.right_shift(turns + 32, 6), 3)
    rest = jnp.bitwise_and(turns + 32, 63) - 32
    angle = rest.astype(jnp.float32) * (math.pi / 128.0)
    square = angle * angle
    sine = angle + angle * square * (
        -1.6666654611e-1 + square * (8.3321608736e-3 - 1.9515295891e-4 * square)
    )
    cosine = (1.0 - 0.5 * square) + square * square * (
        4.166664568298827e-2
        + square * (-1.388731625493765e-3 + 2.443315711809948e-5 * square)
    )
    odd = jnp.bitwise_and(quadrant, 1) == 1
    first = jnp.where(odd, sine, cosine)
    second = jnp.where(odd, cosine, sine)
    flip_cos = (quadrant == 1) | (quadrant == 2)
    flip_sin = quadrant >= 2
    return jnp.where(flip_cos, -first, first), jnp.where(flip_sin, -second, second)


def split(value):
    high = value.astype(jnp.bfloat16)
    low = (value - high.astype(jnp.float32)).astype(jnp.bfloat16)
    return high, low


def spectra_kernel(
    along_z,
    along_x,
    snap,
    weights,
    bins,
    starts,
    grouped,
    total,
    xbuf,
    table_high,
    table_low,
    x_high,
    x_low,
    coef_high,
    coef_low,
    outbox,
    row_out,
    row_in,
    far_out,
    far_in,
    load_sem,
    mine_sem,
    row_send,
    row_recv,
    far_send,
    far_recv,
    box_send,
    box_recv,
):
    band = lax.axis_index("band")
    space = lax.axis_index("space")
    z_at = space // along_x
    x_at = space % along_x
    bands = SLABS
    plane = along_x * bands
    me = x_at * bands + band

    def plane_peer(step):
        peer = lax.rem(me + step, plane)
        return peer % bands, (peer % bands, z_at * along_x + peer // bands)

    def far_peer(step):
        return (band, lax.rem(z_at + step, along_z) * along_x + x_at)

    piece = TIMES * TILES // CHUNKS
    loads = []
    for part in range(CHUNKS):
        load = pltpu.make_async_copy(
            snap.at[pl.ds(part * piece, piece)],
            xbuf.at[pl.ds(part * piece, piece)],
            load_sem.at[part],
        )
        load.start()
        loads.append(load)

    barrier = pltpu.get_barrier_semaphore()
    for step in range(1, along_z):
        pl.semaphore_signal(barrier, inc=1, device_id=far_peer(step), device_id_type=MESH)
    for step in range(1, plane):
        pl.semaphore_signal(
            barrier, inc=1, device_id=plane_peer(step)[1], device_id_type=MESH
        )

    shape = (2 * NBLK, TIMES)
    row = lax.broadcasted_iota(jnp.int32, shape, 0)
    moment = lax.broadcasted_iota(jnp.int32, shape, 1)
    offset = moment
    for block in range(NBLK):
        offset = jnp.where(
            jnp.bitwise_and(row, NBLK - 1) == block, moment - starts[block], offset
        )
    inside = (offset >= 0) & (offset < BLOCK)
    wave, _ = turn_parts(jnp.bitwise_and(offset, BLOCK - 1))
    scaled = jnp.where(inside, 0.5 - 0.5 * wave, 0.0) / math.sqrt(0.375 * BLOCK)

    def fill(pair, carry):
        bin_of = jnp.where(row < NBLK, bins[2 * pair], bins[2 * pair + 1])
        cosine, sine = turn_parts(jnp.bitwise_and(bin_of * offset, BLOCK - 1))
        at = pl.multiple_of(pair * 2 * NBLK, 2 * NBLK)
        for low_row, value in ((0, scaled * cosine), (HALF, -(scaled * sine))):
            high, low = split(value)
            table_high[pl.ds(low_row + at, 2 * NBLK), :] = high
            table_low[pl.ds(low_row + at, 2 * NBLK), :] = low
        return carry

    lax.fori_loop(0, NFREQ // 2, fill, 0)

    sums = jnp.zeros((32, LANES), jnp.float32)
    for part in range(CHUNKS):
        loads[part].wait()

        def gather(index, acc, part=part):
            at = pl.multiple_of(part * piece + index * 32, 32)
            return acc + xbuf[pl.ds(at, 32), :]

        sums = lax.fori_loop(0, piece // 32, gather, sums, unroll=4)
    sums = (sums[0:8] + sums[8:16]) + (sums[16:24] + sums[24:32])
    mean = (sums[0:4] + sums[4:8]) * (1.0 / TIMES)

    def reduce_mean(index, carry):
        at = pl.multiple_of(index * 32, 32)
        for tile in range(TILES):
            value = xbuf[pl.ds(at * TILES + tile, 32, stride=TILES), :]
            high, low = split(value - mean[tile : tile + 1, :])
            x_high[pl.ds(at, 32), tile * LANES : (tile + 1) * LANES] = high
            x_low[pl.ds(at, 32), tile * LANES : (tile + 1) * LANES] = low
        return carry

    lax.fori_loop(0, TIMES // 32, reduce_mean, 0, unroll=2)

    root = jnp.sqrt(weights[...])
    for side in range(2):
        lanes = slice(side * 256, side * 256 + 256)
        scale = jnp.concatenate(
            [root[2 * side : 2 * side + 1, :], root[2 * side + 1 : 2 * side + 2, :]], axis=1
        )
        coef = jnp.dot(table_high[...], x_high[:, lanes], preferred_element_type=jnp.float32)
        coef += jnp.dot(table_low[...], x_high[:, lanes], preferred_element_type=jnp.float32)
        coef += jnp.dot(table_high[...], x_low[:, lanes], preferred_element_type=jnp.float32)
        coef = coef * scale
        high, low = split(coef)
        coef_high[:, lanes] = high
        coef_low[:, lanes] = low
        for part in range(2):
            for freq in range(NFREQ):
                for tile in range(2):
                    value = coef[
                        part * HALF + freq * NBLK : part * HALF + (freq + 1) * NBLK,
                        tile * LANES : (tile + 1) * LANES,
                    ]
                    base = part * 64 + (freq % 2) * TILES + 2 * side + tile
                    outbox[freq // 2, pl.ds(base, NBLK, stride=8), :] = value

    across = (((1,), (1,)), ((), ()))
    gram = lax.dot_general(
        coef_high[...], coef_high[...], across, preferred_element_type=jnp.float32
    )
    gram += lax.dot_general(
        coef_low[...], coef_high[...], across, preferred_element_type=jnp.float32
    )
    gram += lax.dot_general(
        coef_high[...], coef_low[...], across, preferred_element_type=jnp.float32
    )
    tile_shape = (NBLK, LANES)
    sub = lax.broadcasted_iota(jnp.int32, tile_shape, 0)
    lane = lax.broadcasted_iota(jnp.int32, tile_shape, 1)
    real = jnp.zeros(tile_shape, jnp.float32)
    imag = jnp.zeros(tile_shape, jnp.float32)
    for freq in range(NFREQ):
        up = slice(freq * NBLK, (freq + 1) * NBLK)
        down = slice(HALF + freq * NBLK, HALF + (freq + 1) * NBLK)
        own = jnp.right_shift(lane, 3) == freq
        real = jnp.where(own, gram[up, :HALF] + gram[down, HALF:], real)
        imag = jnp.where(own, gram[up, HALF:] - gram[down, :HALF], imag)
    count = SLABS * CELLS * along_x * along_z
    packed = jnp.where(sub <= jnp.bitwise_and(lane, 7), real, imag) * (1.0 / count)
    diagonal = jnp.right_shift(lane, 4) == sub
    rows = jnp.where(diagonal, packed, 0.0)
    for step in range(1, 8):
        turned = jnp.where(diagonal, pltpu.roll(packed, 16 * step, 1), 0.0)
        rows = rows + pltpu.roll(turned, 8 - step, 0)
    row_out[...] = rows.reshape(NBLK, 1, LANES)
    row_in[me] = row_out[band]

    pl.semaphore_wait(barrier, plane - 1 + along_z - 1)

    row_copies = []
    for step in range(1, plane):
        peer_band, peer = plane_peer(step)
        copy = pltpu.make_async_remote_copy(
            src_ref=row_out.at[peer_band],
            dst_ref=row_in.at[me],
            send_sem=row_send,
            recv_sem=row_recv,
            device_id=peer,
            device_id_type=MESH,
        )
        copy.start()
        row_copies.append(copy)
    mine = pltpu.make_async_copy(outbox.at[band], grouped.at[band], mine_sem)
    mine.start()
    box_copies = []
    for step in (4, 3, 5, 2, 6, 1, 7):
        peer_band = lax.rem(band + step, bands)
        copy = pltpu.make_async_remote_copy(
            src_ref=outbox.at[peer_band],
            dst_ref=grouped.at[band],
            send_sem=box_send,
            recv_sem=box_recv,
            device_id=(peer_band, space),
            device_id_type=MESH,
        )
        copy.start()
        box_copies.append(copy)

    arrived = row_in.at[pl.ds(0, plane - 1)]
    pltpu.make_async_copy(arrived, arrived, row_recv).wait()
    near = jnp.sum(row_in[...], axis=0)
    far_out[...] = near.reshape(1, 1, LANES)
    far_in[z_at] = near

    far_copies = []
    for step in sorted(range(1, along_z), key=lambda s: -min(s, along_z - s)):
        copy = pltpu.make_async_remote_copy(
            src_ref=far_out.at[0],
            dst_ref=far_in.at[z_at],
            send_sem=far_send,
            recv_sem=far_recv,
            device_id=far_peer(step),
            device_id_type=MESH,
        )
        copy.start()
        far_copies.append(copy)
    pltpu.make_async_copy(arrived, arrived, row_send).wait()
    arrived = far_in.at[pl.ds(0, along_z - 1)]
    pltpu.make_async_copy(arrived, arrived, far_recv).wait()
    total[...] = jnp.broadcast_to(jnp.sum(far_in[...], axis=0), (8, LANES))
    pltpu.make_async_copy(arrived, arrived, far_send).wait()
    mine.wait()
    arrived = grouped.at[pl.ds(0, bands - 1)]
    pltpu.make_async_copy(arrived, arrived, box_recv).wait()
    arrived = outbox.at[pl.ds(0, bands - 1)]
    pltpu.make_async_copy(arrived, arrived, box_send).wait()


def modes_kernel(total, grouped, factor, modes, held, out_sem):
    shape = (NBLK, LANES)
    sub = lax.broadcasted_iota(jnp.int32, shape, 0)
    lane = lax.broadcasted_iota(jnp.int32, shape, 1)
    packed = total[...]
    packed = jnp.where(sub < 4, packed, pltpu.roll(packed, LANES - 8, 1))

    def entry(r, c):
        return jnp.broadcast_to(packed[:, 16 * r + c : 16 * r + c + 1], shape)

    order = NBLK
    gram_real = {(r, c): entry(r, c) for r in range(order) for c in range(r, order)}
    gram_imag = {(r, c): -entry(c, r) for r in range(order) for c in range(r + 1, order)}
    inv_real, inv_imag = {}, {}
    fac = [jnp.zeros(shape, jnp.float32), jnp.zeros(shape, jnp.float32)]
    copies = []
    for k in range(order):
        pivot = gram_real[k, k]
        scale = lax.rsqrt(pivot)
        scale = scale * (1.5 - 0.5 * pivot * scale * scale)
        row_real, row_imag = {}, {}
        for c in range(k + 1, order):
            row_real[c] = gram_real[k, c] * scale
            row_imag[c] = gram_imag[k, c] * scale
        fac[0] = jnp.where(lane == 8 * k + k, pivot * scale, fac[0])
        for c in range(k + 1, order):
            fac[0] = jnp.where(lane == 8 * k + c, row_real[c], fac[0])
            fac[1] = jnp.where(lane == 8 * k + c, row_imag[c], fac[1])
        for i in range(k + 1, order):
            gram_real[i, i] = gram_real[i, i] - (
                row_real[i] * row_real[i] + row_imag[i] * row_imag[i]
            )
            for c in range(i + 1, order):
                gram_real[i, c] = gram_real[i, c] - (
                    row_real[i] * row_real[c] + row_imag[i] * row_imag[c]
                )
                gram_imag[i, c] = gram_imag[i, c] - (
                    row_real[i] * row_imag[c] - row_imag[i] * row_real[c]
                )
        for m in range(k):
            inv_real[k, m] = inv_real[k, m] * scale
            inv_imag[k, m] = inv_imag[k, m] * scale
        inv_real[k, k] = scale
        for i in range(k + 1, order):
            for m in range(k):
                inv_real[i, m] = inv_real[i, m] - (
                    row_real[i] * inv_real[k, m] + row_imag[i] * inv_imag[k, m]
                )
                inv_imag[i, m] = inv_imag[i, m] - (
                    row_real[i] * inv_imag[k, m] - row_imag[i] * inv_real[k, m]
                )
            inv_real[i, k] = -(row_real[i] * scale)
            inv_imag[i, k] = row_imag[i] * scale
        for slab in range(SLABS):
            real = inv_real[k, k] * grouped[slab, pl.ds(k * 8, 8), :]
            imag = inv_real[k, k] * grouped[slab, pl.ds(64 + k * 8, 8), :]
            for a in range(k):
                part_real = grouped[slab, pl.ds(a * 8, 8), :]
                part_imag = grouped[slab, pl.ds(64 + a * 8, 8), :]
                real = real + (inv_real[k, a] * part_real + inv_imag[k, a] * part_imag)
                imag = imag + (inv_real[k, a] * part_imag - inv_imag[k, a] * part_real)
            held[k, pl.ds(slab, 8, stride=8), :] = real
            held[8 + k, pl.ds(slab, 8, stride=8), :] = imag
        for p in range(2):
            for f in range(2):
                copy = pltpu.make_async_copy(
                    held.at[p * 8 + k, pl.ds(f * 32, 32)],
                    modes.at[f, p * 8 + k],
                    out_sem.at[k * 4 + p * 2 + f],
                )
                copy.start()
                copies.append(copy)
    for p in range(2):
        for f in range(2):
            line = jnp.broadcast_to(fac[p][4 * f : 4 * f + 1, :], shape)
            tile = line
            for r in range(1, order):
                tile = jnp.where(sub == r, pltpu.roll(line, LANES - 8 * r, 1), tile)
            factor[f, p] = tile[:, :8]
    for copy in copies:
        copy.wait()


def shards(along_z, along_x, snapshots, quad_weights, freq_bins, block_starts):
    f32, bf16 = jnp.float32, jnp.bfloat16
    vmem = pltpu.VMEM
    dma = pltpu.SemaphoreType.DMA
    bands = SLABS
    grouped, total = pl.pallas_call(
        functools.partial(spectra_kernel, along_z, along_x),
        out_shape=(
            jax.ShapeDtypeStruct((bands, 128, LANES), f32),
            jax.ShapeDtypeStruct((8, LANES), f32),
        ),
        in_specs=[
            pl.BlockSpec(memory_space=pl.ANY),
            pl.BlockSpec(memory_space=pltpu.VMEM),
            pl.BlockSpec(memory_space=pltpu.SMEM),
            pl.BlockSpec(memory_space=pltpu.SMEM),
        ],
        out_specs=(
            pl.BlockSpec(memory_space=pl.ANY),
            pl.BlockSpec(memory_space=pltpu.VMEM),
        ),
        scratch_shapes=[
            vmem((TIMES * TILES, LANES), f32),
            vmem((ROWS, TIMES), bf16),
            vmem((ROWS, TIMES), bf16),
            vmem((TIMES, CELLS), bf16),
            vmem((TIMES, CELLS), bf16),
            vmem((ROWS, CELLS), bf16),
            vmem((ROWS, CELLS), bf16),
            vmem((bands, 128, LANES), f32),
            vmem((bands, 1, LANES), f32),
            vmem((along_x * bands, 1, LANES), f32),
            vmem((1, 1, LANES), f32),
            vmem((along_z, 1, LANES), f32),
            dma((CHUNKS,)),
            dma,
            dma,
            dma,
            dma,
            dma,
            dma,
            dma,
        ],
        compiler_params=pltpu.CompilerParams(collective_id=0, has_side_effects=True),
        name="spectra",
    )(
        snapshots.reshape(TIMES * TILES, LANES),
        quad_weights.reshape(TILES, LANES),
        freq_bins,
        block_starts,
    )
    factor, modes = pl.pallas_call(
        modes_kernel,
        out_shape=(
            jax.ShapeDtypeStruct((2, 2, NBLK, NBLK), f32),
            jax.ShapeDtypeStruct((2, 16, 32, LANES), f32),
        ),
        in_specs=[
            pl.BlockSpec(memory_space=pltpu.VMEM),
            pl.BlockSpec(memory_space=pltpu.VMEM),
        ],
        out_specs=(
            pl.BlockSpec(memory_space=pltpu.VMEM),
            pl.BlockSpec(memory_space=pl.ANY),
        ),
        scratch_shapes=[vmem((16, 64, LANES), f32), dma((32,))],
        name="modes",
    )(total, grouped)
    modes = modes.reshape(2, 2, NBLK, TILES, SLABS, LANES).transpose(0, 1, 2, 4, 3, 5)
    return (factor, modes.reshape(2, 2, NBLK, SLABS, CELLS))


def solution(mesh):
    along_x = min(ALONG_X, mesh.shape["space"])
    along_z = mesh.shape["space"] // along_x
    placed = (P(None, "band", "space"), P("band", "space"), P(), P())
    return jax.shard_map(
        functools.partial(shards, along_z, along_x),
        mesh=mesh,
        in_specs=placed,
        out_specs=(P("band", None, None, None), P("band", None, None, None, "space")),
        check_vma=False,
    )
```

time: 95.4 us -> 33.5 us (0.35)
  the two profiles are of different devices: /device:TPU:8 before, /device:TPU:1 now
where the time goes in v1:
time: 33.5 us; the launch traced here: 33.3 us
  Pallas kernels  32.7 us (98%)
  between operations  0.64 us (2%)
    pallas_call x1, Pallas kernels, shards(): pl.pallas_call(functools.partial(spectra_kernel, along_z, along_x), out_s...  29.5 us
    pallas_call x1, Pallas kernels, shards(): pl.pallas_call(modes_kernel, out_shape=(jax.ShapeDtypeStruct((2, 2, NBLK,...  3.21 us

profile of v1, /device:TPU:1, one launch (start us, length us, event | category | flops | bytes accessed | tf_op | source)
XLA Modules:
  0.0 33.3 jit_solution(17146631870643988064)
XLA Ops:
  0.6 29.5 %spectra.1 = (f32[8,128,128]{2,1,0:T(8,128)}, f32[8,128]{1,0:T(8,128)}) custom-call(f32[4608,128]{1,0:T(8,128)} %bitcast.7, f32[4,128]{1,0:T(4,128)} %bitcast.8, s32[16]{0:T(128)} %bins.1, s32[8]{0:T(128)} %starts.1), custom_call_target="tpu_custom_call" | custom-call | tf_op jit(solution)/shard_map/spectra/pallas_call | solution.py:366
  30.1 3.2 %modes.1 = (f32[2,2,8,8]{3,2,1,0:T(8,128)}, f32[2,16,32,128]{3,2,1,0:T(8,128)}) custom-call(f32[8,128]{1,0:T(8,128)} %get-tuple-element.6.total, f32[8,128,128]{2,1,0:T(8,128)} %get-tuple-element.7.grouped), custom_call_target="tpu_custom_call" | custom-call | tf_op jit(solution)/shard_map/modes/pallas_call | solution.py:412

commit v2 on v1

--- a/solution.py
+++ b/solution.py
@@ -53,11 +53,14 @@
     along_z,
     along_x,
     snap,
+    weights_any,
+    bins_any,
+    starts_any,
+    grouped,
+    total,
     weights,
     bins,
     starts,
-    grouped,
-    total,
     xbuf,
     table_high,
     table_low,
@@ -71,6 +74,7 @@
     far_out,
     far_in,
     load_sem,
+    small_sem,
     mine_sem,
     row_send,
     row_recv,
@@ -87,13 +91,34 @@
     plane = along_x * bands
     me = x_at * bands + band
 
-    def plane_peer(step):
-        peer = lax.rem(me + step, plane)
-        return peer % bands, (peer % bands, z_at * along_x + peer // bands)
+    def plane_peer(dx, dy, dc):
+        x_to = lax.rem(x_at + dx, along_x)
+        band_to = lax.rem(band // 2 + dy, bands // 2) * 2 + lax.rem(band % 2 + dc, 2)
+        return band_to, (band_to, z_at * along_x + x_to)
 
     def far_peer(step):
         return (band, lax.rem(z_at + step, along_z) * along_x + x_at)
 
+    def hops(step, size):
+        return min(step, size - step)
+
+    plane_steps = [
+        (dx, dy, dc)
+        for dx in range(along_x)
+        for dy in range(bands // 2)
+        for dc in range(2)
+        if dx + dy + dc > 0
+    ]
+    plane_steps.sort(key=lambda s: -hops(s[0], along_x) - hops(s[1], bands // 2))
+    far_steps = sorted(range(1, along_z), key=lambda s: -hops(s, along_z))
+
+    smalls = []
+    for index, (source, target) in enumerate(
+        ((starts_any, starts), (bins_any, bins), (weights_any, weights))
+    ):
+        load = pltpu.make_async_copy(source, target, small_sem.at[index])
+        load.start()
+        smalls.append(load)
     piece = TIMES * TILES // CHUNKS
     loads = []
     for part in range(CHUNKS):
@@ -106,12 +131,14 @@
         loads.append(load)
 
     barrier = pltpu.get_barrier_semaphore()
-    for step in range(1, along_z):
+    for step in far_steps:
         pl.semaphore_signal(barrier, inc=1, device_id=far_peer(step), device_id_type=MESH)
-    for step in range(1, plane):
+    for step in plane_steps:
         pl.semaphore_signal(
-            barrier, inc=1, device_id=plane_peer(step)[1], device_id_type=MESH
-        )
+            barrier, inc=1, device_id=plane_peer(*step)[1], device_id_type=MESH
+        )
+    for load in smalls:
+        load.wait()
 
     shape = (2 * NBLK, TIMES)
     row = lax.broadcasted_iota(jnp.int32, shape, 0)
@@ -217,8 +244,8 @@
     pl.semaphore_wait(barrier, plane - 1 + along_z - 1)
 
     row_copies = []
-    for step in range(1, plane):
-        peer_band, peer = plane_peer(step)
+    for step in plane_steps:
+        peer_band, peer = plane_peer(*step)
         copy = pltpu.make_async_remote_copy(
             src_ref=row_out.at[peer_band],
             dst_ref=row_in.at[me],
@@ -252,7 +279,7 @@
     far_in[z_at] = near
 
     far_copies = []
-    for step in sorted(range(1, along_z), key=lambda s: -min(s, along_z - s)):
+    for step in far_steps:
         copy = pltpu.make_async_remote_copy(
             src_ref=far_out.at[0],
             dst_ref=far_in.at[z_at],
@@ -275,7 +302,7 @@
     pltpu.make_async_copy(arrived, arrived, box_send).wait()
 
 
-def modes_kernel(total, grouped, factor, modes, held, out_sem):
+def modes_kernel(total, grouped, factor, modes, tiles, held, tile_sem, out_sem):
     shape = (NBLK, LANES)
     sub = lax.broadcasted_iota(jnp.int32, shape, 0)
     lane = lax.broadcasted_iota(jnp.int32, shape, 1)
@@ -336,26 +363,27 @@
                 part_imag = grouped[slab, pl.ds(64 + a * 8, 8), :]
                 real = real + (inv_real[k, a] * part_real + inv_imag[k, a] * part_imag)
                 imag = imag + (inv_real[k, a] * part_imag - inv_imag[k, a] * part_real)
-            held[k, pl.ds(slab, 8, stride=8), :] = real
-            held[8 + k, pl.ds(slab, 8, stride=8), :] = imag
-        for p in range(2):
-            for f in range(2):
-                copy = pltpu.make_async_copy(
-                    held.at[p * 8 + k, pl.ds(f * 32, 32)],
-                    modes.at[f, p * 8 + k],
-                    out_sem.at[k * 4 + p * 2 + f],
-                )
-                copy.start()
-                copies.append(copy)
-    for p in range(2):
+            held[k, 0, pl.ds(slab, 8, stride=8), :] = real
+            held[k, 1, pl.ds(slab, 8, stride=8), :] = imag
+        if k == order - 1:
+            for p in range(2):
+                for f in range(2):
+                    line = jnp.broadcast_to(fac[p][4 * f : 4 * f + 1, :], shape)
+                    tile = line
+                    for r in range(1, order):
+                        tile = jnp.where(sub == r, pltpu.roll(line, LANES - 8 * r, 1), tile)
+                    tiles[f, p] = tile[:, :8]
+            out = pltpu.make_async_copy(tiles, factor, tile_sem)
+            out.start()
         for f in range(2):
-            line = jnp.broadcast_to(fac[p][4 * f : 4 * f + 1, :], shape)
-            tile = line
-            for r in range(1, order):
-                tile = jnp.where(sub == r, pltpu.roll(line, LANES - 8 * r, 1), tile)
-            factor[f, p] = tile[:, :8]
-    for copy in copies:
-        copy.wait()
+            copy = pltpu.make_async_copy(
+                held.at[k, :, pl.ds(f * 32, 32)],
+                modes.at[f, :, k],
+                out_sem,
+            )
+            copy.start()
+    out.wait()
+    pltpu.make_async_copy(modes, modes, out_sem).wait()
 
 
 def shards(along_z, along_x, snapshots, quad_weights, freq_bins, block_starts):
@@ -366,20 +394,15 @@
     grouped, total = pl.pallas_call(
         functools.partial(spectra_kernel, along_z, along_x),
         out_shape=(
-            jax.ShapeDtypeStruct((bands, 128, LANES), f32),
-            jax.ShapeDtypeStruct((8, LANES), f32),
+            vmem((bands, 128, LANES), f32),
+            vmem((8, LANES), f32),
         ),
-        in_specs=[
-            pl.BlockSpec(memory_space=pl.ANY),
-            pl.BlockSpec(memory_space=pltpu.VMEM),
-            pl.BlockSpec(memory_space=pltpu.SMEM),
-            pl.BlockSpec(memory_space=pltpu.SMEM),
-        ],
-        out_specs=(
-            pl.BlockSpec(memory_space=pl.ANY),
-            pl.BlockSpec(memory_space=pltpu.VMEM),
-        ),
+        in_specs=[pl.BlockSpec(memory_space=pl.ANY)] * 4,
+        out_specs=(pl.BlockSpec(memory_space=pltpu.VMEM), pl.BlockSpec(memory_space=pltpu.VMEM)),
         scratch_shapes=[
+            vmem((TILES, LANES), f32),
+            pltpu.SMEM((NFREQ,), jnp.int32),
+            pltpu.SMEM((NBLK,), jnp.int32),
             vmem((TIMES * TILES, LANES), f32),
             vmem((ROWS, TIMES), bf16),
             vmem((ROWS, TIMES), bf16),
@@ -393,6 +416,7 @@
             vmem((1, 1, LANES), f32),
             vmem((along_z, 1, LANES), f32),
             dma((CHUNKS,)),
+            dma((3,)),
             dma,
             dma,
             dma,
@@ -413,19 +437,27 @@
         modes_kernel,
         out_shape=(
             jax.ShapeDtypeStruct((2, 2, NBLK, NBLK), f32),
-            jax.ShapeDtypeStruct((2, 16, 32, LANES), f32),
+            jax.ShapeDtypeStruct((2, 2, NBLK, 32, LANES), f32),
         ),
         in_specs=[
             pl.BlockSpec(memory_space=pltpu.VMEM),
             pl.BlockSpec(memory_space=pltpu.VMEM),
         ],
         out_specs=(
-            pl.BlockSpec(memory_space=pltpu.VMEM),
+            pl.BlockSpec(memory_space=pl.ANY),
             pl.BlockSpec(memory_space=pl.ANY),
         ),
-        scratch_shapes=[vmem((16, 64, LANES), f32), dma((32,))],
+        scratch_shapes=[
+            vmem((2, 2, NBLK, NBLK), f32),
+            vmem((NBLK, 2, 64, LANES), f32),
+            dma,
+            dma,
+        ],
         name="modes",
-    )(total, grouped)
+    )(
+        pltpu.with_memory_space_constraint(total, pltpu.VMEM),
+        pltpu.with_memory_space_constraint(grouped, pltpu.VMEM),
+    )
     modes = modes.reshape(2, 2, NBLK, TILES, SLABS, LANES).transpose(0, 1, 2, 4, 3, 5)
     return (factor, modes.reshape(2, 2, NBLK, SLABS, CELLS))
 

time: 33.5 us -> 30.6 us (0.913)
  Pallas kernels: 32.7 us -> 29.8 us
    pallas_call x1, Pallas kernels: 3.21 us -> 1.31 us  [shards(): pl.pallas_call(modes_kernel, out_shape=(jax.ShapeDtypeStruct((2, 2, NBLK,...]
    pallas_call x1, Pallas kernels: 29.5 us -> 28.5 us  [shards(): pl.pallas_call(functools.partial(spectra_kernel, along_z, along_x), out_s...]
where the time goes in v2:
time: 30.6 us; the launch traced here: 30.5 us
  Pallas kernels  29.8 us (97%)
  between operations  0.64 us (2%)
    pallas_call x1, Pallas kernels, shards(): pl.pallas_call(functools.partial(spectra_kernel, along_z, along_x), out_s...  28.5 us
    pallas_call x1, Pallas kernels, shards(): pl.pallas_call(modes_kernel, out_shape=(jax.ShapeDtypeStruct((2, 2, NBLK,...  1.31 us

profile of v2, /device:TPU:1, one launch (start us, length us, event | category | flops | bytes accessed | tf_op | source)
XLA Modules:
  0.0 30.5 jit_solution(8588859196617993767)
XLA Ops:
  0.6 28.5 %spectra.1 = (f32[8,128,128]{2,1,0:T(8,128)S(1)}, f32[8,128]{1,0:T(8,128)S(1)}) custom-call(f32[4608,128]{1,0:T(8,128)} %bitcast.7, f32[4,128]{1,0:T(4,128)} %bitcast.8, s32[16]{0:T(128)} %bins_any.1, s32[8]{0:T(128)} %starts_any.1), custom_call_target="tpu_custom_call" | custom-call | tf_op jit(solution)/shard_map/spectra/pallas_call | solution.py:394
  29.2 1.3 %modes.1 = (f32[2,2,8,8]{3,2,1,0:T(8,128)}, f32[2,2,8,32,128]{4,3,2,1,0:T(8,128)}) custom-call(f32[8,128]{1,0:T(8,128)S(1)} %get-tuple-element.6.total, f32[8,128,128]{2,1,0:T(8,128)S(1)} %get-tuple-element.7.grouped), custom_call_target="tpu_custom_call" | custom-call | tf_op jit(solution)/shard_map/modes/pallas_call | solution.py:436

commit v3 on v2

--- a/solution.py
+++ b/solution.py
@@ -20,7 +20,20 @@
 HALF = NFREQ * NBLK
 ALONG_X = 4
 MESH = pl.DeviceIdType.MESH
-CHUNKS = 4
+DEPTH = 256
+STEPS = tuple((at, min(DEPTH, TIMES - at)) for at in range(0, TIMES, DEPTH))
+LAST = TIMES - BLOCK
+LEAST, MOST = 64, 192
+
+
+def reach(block):
+    first = max(LEAST * block, LAST - MOST * (NBLK - 1 - block))
+    final = min(MOST * block, LAST - LEAST * (NBLK - 1 - block))
+    return first, final + BLOCK
+
+
+def active(at, size):
+    return [b for b in range(NBLK) if reach(b)[0] < at + size and reach(b)[1] > at]
 
 
 def turn_parts(turns):
@@ -62,10 +75,10 @@
     bins,
     starts,
     xbuf,
-    table_high,
-    table_low,
+    tables,
     x_high,
     x_low,
+    coef_sum,
     coef_high,
     coef_low,
     outbox,
@@ -82,6 +95,7 @@
     far_recv,
     box_send,
     box_recv,
+    met_sem,
 ):
     band = lax.axis_index("band")
     space = lax.axis_index("space")
@@ -110,7 +124,10 @@
         if dx + dy + dc > 0
     ]
     plane_steps.sort(key=lambda s: -hops(s[0], along_x) - hops(s[1], bands // 2))
+    relay = max(1, along_z // 4)
     far_steps = sorted(range(1, along_z), key=lambda s: -hops(s, along_z))
+
+    near_steps = [step for step in far_steps if hops(step, along_z) <= relay]
 
     smalls = []
     for index, (source, target) in enumerate(
@@ -119,19 +136,15 @@
         load = pltpu.make_async_copy(source, target, small_sem.at[index])
         load.start()
         smalls.append(load)
-    piece = TIMES * TILES // CHUNKS
     loads = []
-    for part in range(CHUNKS):
-        load = pltpu.make_async_copy(
-            snap.at[pl.ds(part * piece, piece)],
-            xbuf.at[pl.ds(part * piece, piece)],
-            load_sem.at[part],
-        )
+    for index, (at, size) in enumerate(STEPS):
+        part = pl.ds(at * TILES, size * TILES)
+        load = pltpu.make_async_copy(snap.at[part], xbuf.at[part], load_sem.at[index])
         load.start()
         loads.append(load)
 
     barrier = pltpu.get_barrier_semaphore()
-    for step in far_steps:
+    for step in near_steps:
         pl.semaphore_signal(barrier, inc=1, device_id=far_peer(step), device_id_type=MESH)
     for step in plane_steps:
         pl.semaphore_signal(
@@ -140,97 +153,158 @@
     for load in smalls:
         load.wait()
 
-    shape = (2 * NBLK, TIMES)
-    row = lax.broadcasted_iota(jnp.int32, shape, 0)
-    moment = lax.broadcasted_iota(jnp.int32, shape, 1)
-    offset = moment
-    for block in range(NBLK):
-        offset = jnp.where(
-            jnp.bitwise_and(row, NBLK - 1) == block, moment - starts[block], offset
-        )
-    inside = (offset >= 0) & (offset < BLOCK)
-    wave, _ = turn_parts(jnp.bitwise_and(offset, BLOCK - 1))
-    scaled = jnp.where(inside, 0.5 - 0.5 * wave, 0.0) / math.sqrt(0.375 * BLOCK)
-
-    def fill(pair, carry):
-        bin_of = jnp.where(row < NBLK, bins[2 * pair], bins[2 * pair + 1])
-        cosine, sine = turn_parts(jnp.bitwise_and(bin_of * offset, BLOCK - 1))
-        at = pl.multiple_of(pair * 2 * NBLK, 2 * NBLK)
-        for low_row, value in ((0, scaled * cosine), (HALF, -(scaled * sine))):
-            high, low = split(value)
-            table_high[pl.ds(low_row + at, 2 * NBLK), :] = high
-            table_low[pl.ds(low_row + at, 2 * NBLK), :] = low
-        return carry
-
-    lax.fori_loop(0, NFREQ // 2, fill, 0)
-
-    sums = jnp.zeros((32, LANES), jnp.float32)
-    for part in range(CHUNKS):
-        loads[part].wait()
-
-        def gather(index, acc, part=part):
-            at = pl.multiple_of(part * piece + index * 32, 32)
-            return acc + xbuf[pl.ds(at, 32), :]
-
-        sums = lax.fori_loop(0, piece // 32, gather, sums, unroll=4)
-    sums = (sums[0:8] + sums[8:16]) + (sums[16:24] + sums[24:32])
-    mean = (sums[0:4] + sums[4:8]) * (1.0 / TIMES)
-
-    def reduce_mean(index, carry):
-        at = pl.multiple_of(index * 32, 32)
+    wide = (16, DEPTH)
+    sub16 = lax.broadcasted_iota(jnp.int32, wide, 0)
+    place = lax.broadcasted_iota(jnp.int32, wide, 1)
+    bin_of = jnp.zeros(wide, jnp.int32)
+    for freq in range(NFREQ):
+        bin_of = jnp.where(sub16 == (freq % 2) * 8 + freq // 2, bins[freq], bin_of)
+    wave, _ = turn_parts(place)
+    scaled = (0.5 - 0.5 * wave) / math.sqrt(0.375 * BLOCK)
+    cosine, sine = turn_parts(jnp.bitwise_and(bin_of * place, BLOCK - 1))
+    base = jnp.concatenate([scaled * cosine, -(scaled * sine)], axis=0)
+    moment = lax.broadcasted_iota(jnp.int32, (32, DEPTH), 1)
+    turned = [pltpu.roll(base, jnp.bitwise_and(starts[b], DEPTH - 1), 1) for b in range(NBLK)]
+    for index, (at, size) in enumerate(STEPS):
+        for order, block in enumerate(active(at, size)):
+            offset = moment + (at - starts[block])
+            value = jnp.where((offset >= 0) & (offset < BLOCK), turned[block], 0.0)
+            high, low = split(value[:, :size])
+            if size < DEPTH:
+                high = jnp.concatenate([high, high], axis=1)
+                low = jnp.concatenate([low, jnp.zeros_like(low)], axis=1)
+            tables[index][0, pl.ds(32 * order, 32), :] = high
+            tables[index][1, pl.ds(32 * order, 32), :] = low
+
+    def add_up(at, size):
+        value = xbuf[pl.ds(at * TILES, size * TILES), :]
+        value = jnp.sum(value.reshape(size * TILES // 32, 32, LANES), axis=0)
+        value = (value[0:8] + value[8:16]) + (value[16:24] + value[24:32])
+        return value[0:4] + value[4:8]
+
+    def convert(index, middle):
+        at, size = STEPS[index]
+        for first in range(0, size, 16):
+            for tile in range(TILES):
+                lanes = slice(tile * LANES, (tile + 1) * LANES)
+                value = xbuf[pl.ds((at + first) * TILES + tile, 16, stride=TILES), :]
+                high, low = split(value - middle[tile : tile + 1, :])
+                x_high[index][pl.ds(first, 16), lanes] = high
+                if size < DEPTH:
+                    x_high[index][pl.ds(size + first, 16), lanes] = low
+                else:
+                    x_low[index][pl.ds(first, 16), lanes] = low
+
+    def work(*flat):
+        sums_of = (flat[:NBLK], flat[NBLK:])
+
+        def transform(index):
+            blocks = active(*STEPS[index])
+            passes = [(x_high[index], (0, 1))]
+            if STEPS[index][1] == DEPTH:
+                passes.append((x_low[index], (0,)))
+            for turn, (source, kinds) in enumerate(passes):
+                for side in range(2):
+                    pltpu.matmul_push_rhs(
+                        source[:, side * 256 : side * 256 + 256], staging_register=turn, mxu_index=side
+                    )
+                for order, block in enumerate(blocks):
+                    for kind in kinds:
+                        rows = tables[index][kind, pl.ds(32 * order, 32), :]
+                        fresh = turn if order == 0 and kind == 0 else None
+                        for side in range(2):
+                            pltpu.matmul_acc_lhs(sums_of[side][block], rows, load_staged_rhs=fresh)
+
+        loads[0].wait()
+        sums = add_up(*STEPS[0])
+        middle = sums * (1.0 / STEPS[0][1])
+        convert(0, middle)
+        for index in range(1, len(STEPS)):
+            loads[index].wait()
+            sums = sums + add_up(*STEPS[index])
+            convert(index, middle)
+            transform(index - 1)
+        transform(len(STEPS) - 1)
+        for block in range(NBLK):
+            for side in range(2):
+                part = pltpu.matmul_pop(sums_of[side][block])
+                for p in range(2):
+                    for f in range(2):
+                        for tile in range(2):
+                            coef_sum[
+                                pl.ds((f * TILES + side * 2 + tile) * 128 + block * 16 + p * 8, 8), :
+                            ] = part[
+                                p * 16 + f * 8 : p * 16 + f * 8 + 8,
+                                tile * LANES : (tile + 1) * LANES,
+                            ]
+        tile_shape = (NBLK, LANES)
+        sub = lax.broadcasted_iota(jnp.int32, tile_shape, 0)
+        lane = lax.broadcasted_iota(jnp.int32, tile_shape, 1)
+        lean = (sums * (1.0 / TIMES) - middle) * (BLOCK / 4 / math.sqrt(0.375 * BLOCK))
+        root = jnp.sqrt(weights[...])
+        root_pair = jnp.concatenate([root, root], axis=0)
+        lean_pair = jnp.concatenate([lean, jnp.zeros_like(lean)], axis=0)
         for tile in range(TILES):
-            value = xbuf[pl.ds(at * TILES + tile, 32, stride=TILES), :]
-            high, low = split(value - mean[tile : tile + 1, :])
-            x_high[pl.ds(at, 32), tile * LANES : (tile + 1) * LANES] = high
-            x_low[pl.ds(at, 32), tile * LANES : (tile + 1) * LANES] = low
-        return carry
-
-    lax.fori_loop(0, TIMES // 32, reduce_mean, 0, unroll=2)
-
-    root = jnp.sqrt(weights[...])
-    for side in range(2):
-        lanes = slice(side * 256, side * 256 + 256)
-        scale = jnp.concatenate(
-            [root[2 * side : 2 * side + 1, :], root[2 * side + 1 : 2 * side + 2, :]], axis=1
-        )
-        coef = jnp.dot(table_high[...], x_high[:, lanes], preferred_element_type=jnp.float32)
-        coef += jnp.dot(table_low[...], x_high[:, lanes], preferred_element_type=jnp.float32)
-        coef += jnp.dot(table_high[...], x_low[:, lanes], preferred_element_type=jnp.float32)
-        coef = coef * scale
-        high, low = split(coef)
-        coef_high[:, lanes] = high
-        coef_low[:, lanes] = low
-        for part in range(2):
-            for freq in range(NFREQ):
-                for tile in range(2):
-                    value = coef[
-                        part * HALF + freq * NBLK : part * HALF + (freq + 1) * NBLK,
-                        tile * LANES : (tile + 1) * LANES,
-                    ]
-                    base = part * 64 + (freq % 2) * TILES + 2 * side + tile
-                    outbox[freq // 2, pl.ds(base, NBLK, stride=8), :] = value
-
-    across = (((1,), (1,)), ((), ()))
-    gram = lax.dot_general(
-        coef_high[...], coef_high[...], across, preferred_element_type=jnp.float32
-    )
-    gram += lax.dot_general(
-        coef_low[...], coef_high[...], across, preferred_element_type=jnp.float32
-    )
-    gram += lax.dot_general(
-        coef_high[...], coef_low[...], across, preferred_element_type=jnp.float32
-    )
+            lanes = slice(tile * LANES, (tile + 1) * LANES)
+            for p in range(2):
+                for pair in range(NFREQ // 2):
+                    values = []
+                    for f in range(2):
+                        at = (f * TILES + tile) * 128 + p * 8 + pair
+                        value = coef_sum[pl.ds(at, NBLK, stride=16), :]
+                        if p == 0 and pair == 0 and f == 0:
+                            value = value + lean[tile : tile + 1, :]
+                        values.append(value * root[tile : tile + 1, :])
+                    high, low = split(jnp.concatenate(values, axis=0))
+                    to = pl.ds(p * HALF + pair * 16, 16)
+                    coef_high[to, lanes] = high
+                    coef_low[to, lanes] = low
+        for pair in range(NFREQ // 2):
+            for p in range(2):
+                for block in range(NBLK):
+                    value = coef_sum[pl.ds(block * 16 + p * 8 + pair, 8, stride=128), :]
+                    if p == 0 and pair == 0:
+                        value = value + lean_pair
+                    outbox[pl.ds(pair * 128 + p * 64 + block * 8, 8), :] = value * root_pair
+
+        for side in range(2):
+            lanes = slice(side * 256, side * 256 + 256)
+            pltpu.matmul_push_rhs(
+                coef_high[:, lanes], staging_register=0, mxu_index=side, transpose=True
+            )
+            pltpu.matmul_push_rhs(
+                coef_low[:, lanes], staging_register=1, mxu_index=side, transpose=True
+            )
+        for source, rhs in ((coef_high, 0), (coef_low, None), (coef_high, 1)):
+            for part in range(NBLK):
+                for side in range(2):
+                    pltpu.matmul_acc_lhs(
+                        sums_of[side][part],
+                        source[pl.ds(32 * part, 32), side * 256 : side * 256 + 256],
+                        load_staged_rhs=rhs if part == 0 else None,
+                    )
+        gram = [
+            pltpu.matmul_pop(sums_of[0][part]) + pltpu.matmul_pop(sums_of[1][part])
+            for part in range(NBLK)
+        ]
+        real = jnp.zeros(tile_shape, jnp.float32)
+        imag = jnp.zeros(tile_shape, jnp.float32)
+        for freq in range(NFREQ):
+            at = freq % 4 * NBLK
+            up = gram[freq // 4][at : at + NBLK]
+            down = gram[4 + freq // 4][at : at + NBLK]
+            own = jnp.right_shift(lane, 3) == freq
+            real = jnp.where(own, up[:, :HALF] + down[:, HALF:], real)
+            imag = jnp.where(own, up[:, HALF:] - down[:, :HALF], imag)
+        return real, imag
+
+    real, imag = pl.run_scoped(
+        work, *[pltpu.ACC(side)((32, 256), jnp.float32) for side in range(2) for _ in range(NBLK)]
+    )
+
     tile_shape = (NBLK, LANES)
     sub = lax.broadcasted_iota(jnp.int32, tile_shape, 0)
     lane = lax.broadcasted_iota(jnp.int32, tile_shape, 1)
-    real = jnp.zeros(tile_shape, jnp.float32)
-    imag = jnp.zeros(tile_shape, jnp.float32)
-    for freq in range(NFREQ):
-        up = slice(freq * NBLK, (freq + 1) * NBLK)
-        down = slice(HALF + freq * NBLK, HALF + (freq + 1) * NBLK)
-        own = jnp.right_shift(lane, 3) == freq
-        real = jnp.where(own, gram[up, :HALF] + gram[down, HALF:], real)
-        imag = jnp.where(own, gram[up, HALF:] - gram[down, :HALF], imag)
     count = SLABS * CELLS * along_x * along_z
     packed = jnp.where(sub <= jnp.bitwise_and(lane, 7), real, imag) * (1.0 / count)
     diagonal = jnp.right_shift(lane, 4) == sub
@@ -241,7 +315,7 @@
     row_out[...] = rows.reshape(NBLK, 1, LANES)
     row_in[me] = row_out[band]
 
-    pl.semaphore_wait(barrier, plane - 1 + along_z - 1)
+    pl.semaphore_wait(barrier, len(plane_steps) + len(near_steps))
 
     row_copies = []
     for step in plane_steps:
@@ -256,13 +330,15 @@
         )
         copy.start()
         row_copies.append(copy)
-    mine = pltpu.make_async_copy(outbox.at[band], grouped.at[band], mine_sem)
+    mine = pltpu.make_async_copy(
+        outbox.at[pl.ds(pl.multiple_of(band * 128, 128), 128)], grouped.at[band], mine_sem
+    )
     mine.start()
     box_copies = []
     for step in (4, 3, 5, 2, 6, 1, 7):
         peer_band = lax.rem(band + step, bands)
         copy = pltpu.make_async_remote_copy(
-            src_ref=outbox.at[peer_band],
+            src_ref=outbox.at[pl.ds(pl.multiple_of(peer_band * 128, 128), 128)],
             dst_ref=grouped.at[band],
             send_sem=box_send,
             recv_sem=box_recv,
@@ -272,12 +348,17 @@
         copy.start()
         box_copies.append(copy)
 
+    for step in (relay, along_z - relay):
+        pl.semaphore_signal(
+            met_sem, inc=1, device_id=far_peer(step), device_id_type=MESH
+        )
     arrived = row_in.at[pl.ds(0, plane - 1)]
     pltpu.make_async_copy(arrived, arrived, row_recv).wait()
     near = jnp.sum(row_in[...], axis=0)
     far_out[...] = near.reshape(1, 1, LANES)
     far_in[z_at] = near
 
+    pl.semaphore_wait(met_sem, 2)
     far_copies = []
     for step in far_steps:
         copy = pltpu.make_async_remote_copy(
@@ -298,11 +379,11 @@
     mine.wait()
     arrived = grouped.at[pl.ds(0, bands - 1)]
     pltpu.make_async_copy(arrived, arrived, box_recv).wait()
-    arrived = outbox.at[pl.ds(0, bands - 1)]
+    arrived = outbox.at[pl.ds(0, (bands - 1) * 128)]
     pltpu.make_async_copy(arrived, arrived, box_send).wait()
 
 
-def modes_kernel(total, grouped, factor, modes, tiles, held, tile_sem, out_sem):
+def modes_kernel(total, grouped, factor, modes, tiles, mixed, held, tile_sem, out_sem):
     shape = (NBLK, LANES)
     sub = lax.broadcasted_iota(jnp.int32, shape, 0)
     lane = lax.broadcasted_iota(jnp.int32, shape, 1)
@@ -363,8 +444,13 @@
                 part_imag = grouped[slab, pl.ds(64 + a * 8, 8), :]
                 real = real + (inv_real[k, a] * part_real + inv_imag[k, a] * part_imag)
                 imag = imag + (inv_real[k, a] * part_imag - inv_imag[k, a] * part_real)
-            held[k, 0, pl.ds(slab, 8, stride=8), :] = real
-            held[k, 1, pl.ds(slab, 8, stride=8), :] = imag
+            mixed[pl.ds(k * 128 + slab * 8, 8), :] = real
+            mixed[pl.ds(k * 128 + 64 + slab * 8, 8), :] = imag
+        for p in range(2):
+            for row in range(8):
+                held[k, p, pl.ds(row * 8, 8), :] = mixed[
+                    pl.ds(k * 128 + p * 64 + row, 8, stride=8), :
+                ]
         if k == order - 1:
             for p in range(2):
                 for f in range(2):
@@ -404,18 +490,18 @@
             pltpu.SMEM((NFREQ,), jnp.int32),
             pltpu.SMEM((NBLK,), jnp.int32),
             vmem((TIMES * TILES, LANES), f32),
-            vmem((ROWS, TIMES), bf16),
-            vmem((ROWS, TIMES), bf16),
-            vmem((TIMES, CELLS), bf16),
-            vmem((TIMES, CELLS), bf16),
+            [vmem((2, 32 * len(active(*step)), DEPTH), bf16) for step in STEPS],
+            [vmem((DEPTH, CELLS), bf16) for step in STEPS],
+            [vmem((DEPTH, CELLS), bf16) for step in STEPS if step[1] == DEPTH],
+            vmem((ROWS * TILES, LANES), f32),
             vmem((ROWS, CELLS), bf16),
             vmem((ROWS, CELLS), bf16),
-            vmem((bands, 128, LANES), f32),
+            vmem((bands * 128, LANES), f32),
             vmem((bands, 1, LANES), f32),
             vmem((along_x * bands, 1, LANES), f32),
             vmem((1, 1, LANES), f32),
             vmem((along_z, 1, LANES), f32),
-            dma((CHUNKS,)),
+            dma((len(STEPS),)),
             dma((3,)),
             dma,
             dma,
@@ -424,6 +510,7 @@
             dma,
             dma,
             dma,
+            pltpu.SemaphoreType.REGULAR,
         ],
         compiler_params=pltpu.CompilerParams(collective_id=0, has_side_effects=True),
         name="spectra",
@@ -449,6 +536,7 @@
         ),
         scratch_shapes=[
             vmem((2, 2, NBLK, NBLK), f32),
+            vmem((NBLK * 128, LANES), f32),
             vmem((NBLK, 2, 64, LANES), f32),
             dma,
             dma,

time: 30.6 us -> 29.1 us (0.951)
  Pallas kernels: 29.8 us -> 28.4 us
    pallas_call x1, Pallas kernels: 28.5 us -> 27 us  [shards(): pl.pallas_call(functools.partial(spectra_kernel, along_z, along_x), out_s...]
where the time goes in v3:
time: 29.1 us; the launch traced here: 29 us
  Pallas kernels  28.4 us (98%)
  between operations  0.64 us (2%)
    pallas_call x1, Pallas kernels, shards(): pl.pallas_call(functools.partial(spectra_kernel, along_z, along_x), out_s...  27 us
    pallas_call x1, Pallas kernels, shards(): pl.pallas_call(modes_kernel, out_shape=(jax.ShapeDtypeStruct((2, 2, NBLK,...  1.35 us

profile of v3, /device:TPU:1, one launch (start us, length us, event | category | flops | bytes accessed | tf_op | source)
XLA Modules:
  0.0 29.0 jit_solution(5011195091309502854)
XLA Ops:
  0.6 27.0 %spectra.1 = (f32[8,128,128]{2,1,0:T(8,128)S(1)}, f32[8,128]{1,0:T(8,128)S(1)}) custom-call(f32[4608,128]{1,0:T(8,128)} %bitcast.7, f32[4,128]{1,0:T(4,128)} %bitcast.8, s32[16]{0:T(128)} %bins_any.1, s32[8]{0:T(128)} %starts_any.1), custom_call_target="tpu_custom_call" | custom-call | tf_op jit(solution)/shard_map/spectra/pallas_call | solution.py:480
  27.7 1.4 %modes.1 = (f32[2,2,8,8]{3,2,1,0:T(8,128)}, f32[2,2,8,32,128]{4,3,2,1,0:T(8,128)}) custom-call(f32[8,128]{1,0:T(8,128)S(1)} %get-tuple-element.6.total, f32[8,128,128]{2,1,0:T(8,128)S(1)} %get-tuple-element.7.grouped), custom_call_target="tpu_custom_call" | custom-call | tf_op jit(solution)/shard_map/modes/pallas_call | solution.py:523

commit v4 on v3

--- a/solution.py
+++ b/solution.py
@@ -225,47 +225,25 @@
             convert(index, middle)
             transform(index - 1)
         transform(len(STEPS) - 1)
+        lean = (sums * (1.0 / TIMES) - middle) * (BLOCK / 4 / math.sqrt(0.375 * BLOCK))
+        root = jnp.sqrt(weights[...])
+        top = lax.broadcasted_iota(jnp.int32, (32, LANES), 0) == 0
         for block in range(NBLK):
             for side in range(2):
                 part = pltpu.matmul_pop(sums_of[side][block])
-                for p in range(2):
-                    for f in range(2):
-                        for tile in range(2):
-                            coef_sum[
-                                pl.ds((f * TILES + side * 2 + tile) * 128 + block * 16 + p * 8, 8), :
-                            ] = part[
-                                p * 16 + f * 8 : p * 16 + f * 8 + 8,
-                                tile * LANES : (tile + 1) * LANES,
-                            ]
-        tile_shape = (NBLK, LANES)
-        sub = lax.broadcasted_iota(jnp.int32, tile_shape, 0)
-        lane = lax.broadcasted_iota(jnp.int32, tile_shape, 1)
-        lean = (sums * (1.0 / TIMES) - middle) * (BLOCK / 4 / math.sqrt(0.375 * BLOCK))
-        root = jnp.sqrt(weights[...])
-        root_pair = jnp.concatenate([root, root], axis=0)
-        lean_pair = jnp.concatenate([lean, jnp.zeros_like(lean)], axis=0)
-        for tile in range(TILES):
-            lanes = slice(tile * LANES, (tile + 1) * LANES)
-            for p in range(2):
-                for pair in range(NFREQ // 2):
-                    values = []
-                    for f in range(2):
-                        at = (f * TILES + tile) * 128 + p * 8 + pair
-                        value = coef_sum[pl.ds(at, NBLK, stride=16), :]
-                        if p == 0 and pair == 0 and f == 0:
-                            value = value + lean[tile : tile + 1, :]
-                        values.append(value * root[tile : tile + 1, :])
-                    high, low = split(jnp.concatenate(values, axis=0))
-                    to = pl.ds(p * HALF + pair * 16, 16)
-                    coef_high[to, lanes] = high
-                    coef_low[to, lanes] = low
-        for pair in range(NFREQ // 2):
-            for p in range(2):
-                for block in range(NBLK):
-                    value = coef_sum[pl.ds(block * 16 + p * 8 + pair, 8, stride=128), :]
-                    if p == 0 and pair == 0:
-                        value = value + lean_pair
-                    outbox[pl.ds(pair * 128 + p * 64 + block * 8, 8), :] = value * root_pair
+                for half in range(2):
+                    tile = side * 2 + half
+                    lanes = slice(tile * LANES, (tile + 1) * LANES)
+                    value = part[:, half * LANES : (half + 1) * LANES]
+                    value = value + jnp.where(top, lean[tile : tile + 1, :], 0.0)
+                    value = value * root[tile : tile + 1, :]
+                    high, low = split(value)
+                    coef_high[pl.ds(32 * block, 32), lanes] = high
+                    coef_low[pl.ds(32 * block, 32), lanes] = low
+                    for p in range(2):
+                        for f in range(2):
+                            to = pl.ds((f * TILES + tile) * 128 + block * 16 + p * 8, 8)
+                            coef_sum[to, :] = value[p * 16 + f * 8 : p * 16 + f * 8 + 8]
 
         for side in range(2):
             lanes = slice(side * 256, side * 256 + 256)
@@ -287,31 +265,40 @@
             pltpu.matmul_pop(sums_of[0][part]) + pltpu.matmul_pop(sums_of[1][part])
             for part in range(NBLK)
         ]
-        real = jnp.zeros(tile_shape, jnp.float32)
-        imag = jnp.zeros(tile_shape, jnp.float32)
-        for freq in range(NFREQ):
-            at = freq % 4 * NBLK
-            up = gram[freq // 4][at : at + NBLK]
-            down = gram[4 + freq // 4][at : at + NBLK]
-            own = jnp.right_shift(lane, 3) == freq
-            real = jnp.where(own, up[:, :HALF] + down[:, HALF:], real)
-            imag = jnp.where(own, up[:, HALF:] - down[:, :HALF], imag)
-        return real, imag
-
-    real, imag = pl.run_scoped(
+        tile_shape = (NBLK, LANES)
+        sub = lax.broadcasted_iota(jnp.int32, tile_shape, 0)
+        lane = lax.broadcasted_iota(jnp.int32, tile_shape, 1)
+        second = jnp.bitwise_and(lane, 8) != 0
+        own = (jnp.bitwise_and(lane, 7) == sub) & (jnp.bitwise_and(lane, 16) == 0)
+        column = jnp.right_shift(lane, 5)
+        packed = []
+        for half in range(2):
+            lanes = slice(half * LANES, (half + 1) * LANES)
+            total_of = None
+            for block in range(NBLK):
+                part = gram[block][:, lanes]
+                real_row = jnp.where(second, part[8:16], part[0:8])
+                imag_row = jnp.where(second, part[24:32], part[16:24])
+                real_next = pltpu.roll(real_row, LANES - 16, 1)
+                imag_next = pltpu.roll(imag_row, LANES - 16, 1)
+                value = jnp.where(
+                    column + half * 4 >= block, real_row + imag_next, real_next - imag_row
+                )
+                value = jnp.where(own, value, 0.0)
+                if block:
+                    value = pltpu.roll(value, block, 1)
+                total_of = value if total_of is None else total_of + value
+            packed.append(total_of)
+        both = packed[0] + pltpu.roll(packed[1], 16, 1)
+        rows = both
+        for row in range(1, NBLK):
+            rows = jnp.where(sub == row, pltpu.roll(both, LANES - row, 1), rows)
+        return rows
+
+    rows = pl.run_scoped(
         work, *[pltpu.ACC(side)((32, 256), jnp.float32) for side in range(2) for _ in range(NBLK)]
     )
-
-    tile_shape = (NBLK, LANES)
-    sub = lax.broadcasted_iota(jnp.int32, tile_shape, 0)
-    lane = lax.broadcasted_iota(jnp.int32, tile_shape, 1)
-    count = SLABS * CELLS * along_x * along_z
-    packed = jnp.where(sub <= jnp.bitwise_and(lane, 7), real, imag) * (1.0 / count)
-    diagonal = jnp.right_shift(lane, 4) == sub
-    rows = jnp.where(diagonal, packed, 0.0)
-    for step in range(1, 8):
-        turned = jnp.where(diagonal, pltpu.roll(packed, 16 * step, 1), 0.0)
-        rows = rows + pltpu.roll(turned, 8 - step, 0)
+    rows = rows * (1.0 / (SLABS * CELLS * along_x * along_z))
     row_out[...] = rows.reshape(NBLK, 1, LANES)
     row_in[me] = row_out[band]
 
@@ -330,6 +317,16 @@
         )
         copy.start()
         row_copies.append(copy)
+    for step in (relay, along_z - relay):
+        pl.semaphore_signal(
+            met_sem, inc=1, device_id=far_peer(step), device_id_type=MESH
+        )
+    for pair in range(NFREQ // 2):
+        for p in range(2):
+            for block in range(NBLK):
+                outbox[pl.ds(pair * 128 + p * 64 + block * 8, 8), :] = coef_sum[
+                    pl.ds(block * 16 + p * 8 + pair, 8, stride=128), :
+                ]
     mine = pltpu.make_async_copy(
         outbox.at[pl.ds(pl.multiple_of(band * 128, 128), 128)], grouped.at[band], mine_sem
     )
@@ -348,10 +345,6 @@
         copy.start()
         box_copies.append(copy)
 
-    for step in (relay, along_z - relay):
-        pl.semaphore_signal(
-            met_sem, inc=1, device_id=far_peer(step), device_id_type=MESH
-        )
     arrived = row_in.at[pl.ds(0, plane - 1)]
     pltpu.make_async_copy(arrived, arrived, row_recv).wait()
     near = jnp.sum(row_in[...], axis=0)
@@ -372,15 +365,15 @@
         copy.start()
         far_copies.append(copy)
     pltpu.make_async_copy(arrived, arrived, row_send).wait()
-    arrived = far_in.at[pl.ds(0, along_z - 1)]
-    pltpu.make_async_copy(arrived, arrived, far_recv).wait()
-    total[...] = jnp.broadcast_to(jnp.sum(far_in[...], axis=0), (8, LANES))
-    pltpu.make_async_copy(arrived, arrived, far_send).wait()
     mine.wait()
     arrived = grouped.at[pl.ds(0, bands - 1)]
     pltpu.make_async_copy(arrived, arrived, box_recv).wait()
     arrived = outbox.at[pl.ds(0, (bands - 1) * 128)]
     pltpu.make_async_copy(arrived, arrived, box_send).wait()
+    arrived = far_in.at[pl.ds(0, along_z - 1)]
+    pltpu.make_async_copy(arrived, arrived, far_send).wait()
+    pltpu.make_async_copy(arrived, arrived, far_recv).wait()
+    total[...] = jnp.broadcast_to(jnp.sum(far_in[...], axis=0), (8, LANES))
 
 
 def modes_kernel(total, grouped, factor, modes, tiles, mixed, held, tile_sem, out_sem):
@@ -391,7 +384,8 @@
     packed = jnp.where(sub < 4, packed, pltpu.roll(packed, LANES - 8, 1))
 
     def entry(r, c):
-        return jnp.broadcast_to(packed[:, 16 * r + c : 16 * r + c + 1], shape)
+        at = c % 4 * 32 + c // 4 * 16 + r
+        return jnp.broadcast_to(packed[:, at : at + 1], shape)
 
     order = NBLK
     gram_real = {(r, c): entry(r, c) for r in range(order) for c in range(r, order)}

time: 29.1 us -> 29 us (level)
  no operation moved by 1% of the time
where the time goes in v4:
time: 29 us; the launch traced here: 28.9 us
  Pallas kernels  28.2 us (97%)
  between operations  0.64 us (2%)
    pallas_call x1, Pallas kernels, shards(): pl.pallas_call(functools.partial(spectra_kernel, along_z, along_x), out_s...  26.9 us
    pallas_call x1, Pallas kernels, shards(): pl.pallas_call(modes_kernel, out_shape=(jax.ShapeDtypeStruct((2, 2, NBLK,...  1.35 us

profile of v4, /device:TPU:1, one launch (start us, length us, event | category | flops | bytes accessed | tf_op | source)
XLA Modules:
  0.0 28.9 jit_solution(8087546136968594473)
XLA Ops:
  0.6 26.9 %spectra.1 = (f32[8,128,128]{2,1,0:T(8,128)S(1)}, f32[8,128]{1,0:T(8,128)S(1)}) custom-call(f32[4608,128]{1,0:T(8,128)} %bitcast.7, f32[4,128]{1,0:T(4,128)} %bitcast.8, s32[16]{0:T(128)} %bins_any.1, s32[8]{0:T(128)} %starts_any.1), custom_call_target="tpu_custom_call" | custom-call | tf_op jit(solution)/shard_map/spectra/pallas_call | solution.py:474
  27.5 1.4 %modes.1 = (f32[2,2,8,8]{3,2,1,0:T(8,128)}, f32[2,2,8,32,128]{4,3,2,1,0:T(8,128)}) custom-call(f32[8,128]{1,0:T(8,128)S(1)} %get-tuple-element.6.total, f32[8,128,128]{2,1,0:T(8,128)S(1)} %get-tuple-element.7.grouped), custom_call_target="tpu_custom_call" | custom-call | tf_op jit(solution)/shard_map/modes/pallas_call | solution.py:517

commit v5 on v4

--- a/solution.py
+++ b/solution.py
@@ -76,11 +76,7 @@
     starts,
     xbuf,
     tables,
-    x_high,
-    x_low,
     coef_sum,
-    coef_high,
-    coef_low,
     outbox,
     row_out,
     row_in,
@@ -182,83 +178,91 @@
         value = (value[0:8] + value[8:16]) + (value[16:24] + value[24:32])
         return value[0:4] + value[4:8]
 
-    def convert(index, middle):
+    def fetch(index, side, middle):
         at, size = STEPS[index]
+        highs, lows = [], []
         for first in range(0, size, 16):
-            for tile in range(TILES):
-                lanes = slice(tile * LANES, (tile + 1) * LANES)
+            values = []
+            for tile in (2 * side, 2 * side + 1):
                 value = xbuf[pl.ds((at + first) * TILES + tile, 16, stride=TILES), :]
-                high, low = split(value - middle[tile : tile + 1, :])
-                x_high[index][pl.ds(first, 16), lanes] = high
-                if size < DEPTH:
-                    x_high[index][pl.ds(size + first, 16), lanes] = low
-                else:
-                    x_low[index][pl.ds(first, 16), lanes] = low
+                values.append(value - middle[tile : tile + 1, :])
+            high, low = split(jnp.concatenate(values, axis=1))
+            highs.append(high)
+            lows.append(low)
+        if size < DEPTH:
+            return [jnp.concatenate(highs + lows, axis=0)]
+        return [jnp.concatenate(highs, axis=0), jnp.concatenate(lows, axis=0)]
 
     def work(*flat):
         sums_of = (flat[:NBLK], flat[NBLK:])
 
-        def transform(index):
-            blocks = active(*STEPS[index])
-            passes = [(x_high[index], (0, 1))]
-            if STEPS[index][1] == DEPTH:
-                passes.append((x_low[index], (0,)))
-            for turn, (source, kinds) in enumerate(passes):
-                for side in range(2):
-                    pltpu.matmul_push_rhs(
-                        source[:, side * 256 : side * 256 + 256], staging_register=turn, mxu_index=side
-                    )
-                for order, block in enumerate(blocks):
-                    for kind in kinds:
-                        rows = tables[index][kind, pl.ds(32 * order, 32), :]
-                        fresh = turn if order == 0 and kind == 0 else None
-                        for side in range(2):
-                            pltpu.matmul_acc_lhs(sums_of[side][block], rows, load_staged_rhs=fresh)
+        def push(source, register):
+            for side in range(2):
+                pltpu.matmul_push_rhs(source[side], staging_register=register, mxu_index=side)
+
+        def stream(index, kinds, fresh):
+            for order, block in enumerate(active(*STEPS[index])):
+                for kind in kinds:
+                    rows = tables[index][kind, pl.ds(32 * order, 32), :]
+                    for side in range(2):
+                        pltpu.matmul_acc_lhs(sums_of[side][block], rows, load_staged_rhs=fresh)
+                    fresh = None
+
+        coef_parts = {}
+
+        def finish(block):
+            for side in range(2):
+                part = pltpu.matmul_pop(sums_of[side][block])
+                pieces = []
+                for half in range(2):
+                    tile = side * 2 + half
+                    value = part[:, half * LANES : (half + 1) * LANES]
+                    value = value + jnp.where(top, lean[tile : tile + 1, :], 0.0)
+                    value = value * root[tile : tile + 1, :]
+                    pieces.append(value)
+                    for p in range(2):
+                        for f in range(2):
+                            to = pl.ds((f * TILES + tile) * 128 + block * 16 + p * 8, 8)
+                            coef_sum[to, :] = value[p * 16 + f * 8 : p * 16 + f * 8 + 8]
+                coef_parts[side, block] = split(jnp.concatenate(pieces, axis=1))
 
         loads[0].wait()
         sums = add_up(*STEPS[0])
         middle = sums * (1.0 / STEPS[0][1])
-        convert(0, middle)
+        parts = [fetch(0, side, middle) for side in range(2)]
+        push([part[0] for part in parts], 0)
         for index in range(1, len(STEPS)):
+            push([part[1] for part in parts], 1)
+            stream(index - 1, (0, 1), 0)
             loads[index].wait()
             sums = sums + add_up(*STEPS[index])
-            convert(index, middle)
-            transform(index - 1)
-        transform(len(STEPS) - 1)
+            parts = [fetch(index, side, middle) for side in range(2)]
+            push([part[0] for part in parts], 0)
+            stream(index - 1, (0,), 1)
         lean = (sums * (1.0 / TIMES) - middle) * (BLOCK / 4 / math.sqrt(0.375 * BLOCK))
         root = jnp.sqrt(weights[...])
         top = lax.broadcasted_iota(jnp.int32, (32, LANES), 0) == 0
         for block in range(NBLK):
+            if block not in active(*STEPS[-1]):
+                finish(block)
+        stream(len(STEPS) - 1, (0, 1), 0)
+        for block in active(*STEPS[-1]):
+            finish(block)
+
+        def column_of(side, kind):
+            return jnp.concatenate([coef_parts[side, b][kind] for b in range(NBLK)], axis=0)
+
+        for kind in range(2):
             for side in range(2):
-                part = pltpu.matmul_pop(sums_of[side][block])
-                for half in range(2):
-                    tile = side * 2 + half
-                    lanes = slice(tile * LANES, (tile + 1) * LANES)
-                    value = part[:, half * LANES : (half + 1) * LANES]
-                    value = value + jnp.where(top, lean[tile : tile + 1, :], 0.0)
-                    value = value * root[tile : tile + 1, :]
-                    high, low = split(value)
-                    coef_high[pl.ds(32 * block, 32), lanes] = high
-                    coef_low[pl.ds(32 * block, 32), lanes] = low
-                    for p in range(2):
-                        for f in range(2):
-                            to = pl.ds((f * TILES + tile) * 128 + block * 16 + p * 8, 8)
-                            coef_sum[to, :] = value[p * 16 + f * 8 : p * 16 + f * 8 + 8]
-
-        for side in range(2):
-            lanes = slice(side * 256, side * 256 + 256)
-            pltpu.matmul_push_rhs(
-                coef_high[:, lanes], staging_register=0, mxu_index=side, transpose=True
-            )
-            pltpu.matmul_push_rhs(
-                coef_low[:, lanes], staging_register=1, mxu_index=side, transpose=True
-            )
-        for source, rhs in ((coef_high, 0), (coef_low, None), (coef_high, 1)):
+                pltpu.matmul_push_rhs(
+                    column_of(side, kind), staging_register=kind, mxu_index=side, transpose=True
+                )
+        for kind, rhs in ((0, 0), (1, None), (0, 1)):
             for part in range(NBLK):
                 for side in range(2):
                     pltpu.matmul_acc_lhs(
                         sums_of[side][part],
-                        source[pl.ds(32 * part, 32), side * 256 : side * 256 + 256],
+                        coef_parts[side, part][kind],
                         load_staged_rhs=rhs if part == 0 else None,
                     )
         gram = [
@@ -485,11 +489,7 @@
             pltpu.SMEM((NBLK,), jnp.int32),
             vmem((TIMES * TILES, LANES), f32),
             [vmem((2, 32 * len(active(*step)), DEPTH), bf16) for step in STEPS],
-            [vmem((DEPTH, CELLS), bf16) for step in STEPS],
-            [vmem((DEPTH, CELLS), bf16) for step in STEPS if step[1] == DEPTH],
             vmem((ROWS * TILES, LANES), f32),
-            vmem((ROWS, CELLS), bf16),
-            vmem((ROWS, CELLS), bf16),
             vmem((bands * 128, LANES), f32),
             vmem((bands, 1, LANES), f32),
             vmem((along_x * bands, 1, LANES), f32),

time: 29 us -> 28.7 us (0.990)
  Pallas kernels: 28.2 us -> 27.9 us
    pallas_call x1, Pallas kernels: 26.9 us -> 26.6 us  [shards(): pl.pallas_call(functools.partial(spectra_kernel, along_z, along_x), out_s...]
where the time goes in v5:
time: 28.7 us; the launch traced here: 28.6 us
  Pallas kernels  27.9 us (97%)
  between operations  0.64 us (2%)
    pallas_call x1, Pallas kernels, shards(): pl.pallas_call(functools.partial(spectra_kernel, along_z, along_x), out_s...  26.6 us
    pallas_call x1, Pallas kernels, shards(): pl.pallas_call(modes_kernel, out_shape=(jax.ShapeDtypeStruct((2, 2, NBLK,...  1.35 us

profile of v5, /device:TPU:1, one launch (start us, length us, event | category | flops | bytes accessed | tf_op | source)
XLA Modules:
  0.0 28.6 jit_solution(183536502930608126)
XLA Ops:
  0.6 26.6 %spectra.1 = (f32[8,128,128]{2,1,0:T(8,128)S(1)}, f32[8,128]{1,0:T(8,128)S(1)}) custom-call(f32[4608,128]{1,0:T(8,128)} %bitcast.7, f32[4,128]{1,0:T(4,128)} %bitcast.8, s32[16]{0:T(128)} %bins_any.1, s32[8]{0:T(128)} %starts_any.1), custom_call_target="tpu_custom_call" | custom-call | tf_op jit(solution)/shard_map/spectra/pallas_call | solution.py:478
  27.2 1.4 %modes.1 = (f32[2,2,8,8]{3,2,1,0:T(8,128)}, f32[2,2,8,32,128]{4,3,2,1,0:T(8,128)}) custom-call(f32[8,128]{1,0:T(8,128)S(1)} %get-tuple-element.6.total, f32[8,128,128]{2,1,0:T(8,128)S(1)} %get-tuple-element.7.grouped), custom_call_target="tpu_custom_call" | custom-call | tf_op jit(solution)/shard_map/modes/pallas_call | solution.py:517
